TPU v7x, 32 devices: a whole 2x2x4 slice. The times are simulated.
32 devices in a mesh: dp: 16 (over z, y, core), seq: 2 (over x).
Axes of the slice: x: 2, y: 2, z: 4, core: 2. Of those that a mesh axis runs over, the one named last changes fastest.
Arguments:
- hidden_in: bfloat16 [16, 1024, 768], P('dp', 'seq'), may hold values from -18 to 18
- segment_ids: int32 [16, 1024], P('dp'), may hold values from 0 to 7, as said below
- piece_lengths: int32 [16, 8], P('dp'), may hold values from 0 to 1024, as said below
- time_index: int32 [16, 8], P('dp'), may hold values from 0 to 999
- first_gain: float32 [768], replicated, may hold values from 0.5 to 1.5
- modulation_weight: bfloat16 [128, 4608], replicated, may hold values from -0.5 to 0.5
- modulation_bias: float32 [4608], replicated, may hold values from -4 to 4
- query_key_value_weight: bfloat16 [768, 2304], replicated, may hold values from -0.21875 to 0.21875
- attention_output_matrix: bfloat16 [768, 768], replicated, may hold values from -0.875 to 0.875
- second_gain: float32 [768], replicated, may hold values from 0.5 to 1.5
- widen_weight: bfloat16 [768, 3072], replicated, may hold values from -0.21875 to 0.21875
- expand_bias: float32 [3072], replicated, may hold values from -6 to 6
- narrow_weight: bfloat16 [3072, 768], replicated, may hold values from -0.109375 to 0.109375
- reduce_bias: float32 [768], replicated, may hold values from -6 to 6
- cotangent: bfloat16 [16, 1024, 768], P('dp', 'seq'), may hold values from -6 to 6
Outputs:
- block_out: bfloat16 [16, 1024, 768], P('dp', 'seq')
- input_grad: bfloat16 [16, 1024, 768], P('dp', 'seq')
- first_gain_grad: float32 [768], replicated
- modulation_weight_grad: float32 [128, 4608], P('seq', 'dp')
- modulation_bias_grad: float32 [4608], replicated
- triple_weight_grad: float32 [768, 2304], P('seq', 'dp')
- output_weight_grad: float32 [768, 768], P('seq', 'dp')
- second_gain_grad: float32 [768], replicated
- expand_weight_grad: float32 [768, 3072], P('seq', 'dp')
- expand_bias_grad: float32 [3072], replicated
- reduce_weight_grad: float32 [3072, 768], P('seq', 'dp')
- reduce_bias_grad: float32 [768], replicated
- masked_rms: float32 [3], replicated
Inputs may be any that keep to these rules, and one draw needn't show every extreme that they name: `segment_ids`: each slot is cut into equal pieces of 128, 512 or 1024 tokens, the kind drawn for each slot, and a token's segment id is the number of its piece, so ids start at 0 and never fall; the first slot has pieces of 128 and the last one a single piece. piece_lengths[slot, s] counts the valid leading tokens of piece s: more than half of the piece and at most all of it, the first piece of every slot all valid; 0 for numbers beyond the slot's pieces.
All inputs are finite; a program needn't handle non-finite values.
Results may differ from a plain program's by a relative error of at most 0.014.
Values may be sent and summed in bfloat16 or wider, within the bound.
A program may use at most 192 MiB of HBM per device.

v0:
```python
import math
import jax
import jax.numpy as jnp
from jax import lax
from jax.sharding import PartitionSpec as P

HEADS = 12
highest = lax.Precision.HIGHEST
negative = -1000000000.0


def layer_norm(values, scaling):
    centered = values - jnp.mean(values, axis=-1, keepdims=True)
    spread = jnp.mean(centered * centered, axis=-1, keepdims=True)
    return centered * lax.rsqrt(spread + 1e-05) * scaling


def norm_modulate(values, scaling, offset, stretch):
    return layer_norm(values, scaling) * (1.0 + stretch) + offset


def gelu_tanh(values):
    argument = 0.7978845608028654 * (values + 0.044715 * values * values * values)
    return 0.5 * values * (1.0 + jnp.tanh(argument))


def rotate(values, cosine, sine_part):
    halfway = values.shape[-1] // 2
    turned = jnp.concatenate([-values[..., halfway:], values[..., :halfway]], axis=-1)
    return values * cosine + turned * sine_part


def rotary_tables(positions, head_dim):
    freq_index = jnp.arange(head_dim // 2).astype(jnp.float32)
    frequencies = jnp.exp(freq_index * (-2.0 * math.log(10000.0) / head_dim))
    angles = positions[..., None] * frequencies
    angles = jnp.concatenate([angles, angles], axis=-1)
    return (jnp.cos(angles)[..., None, :], jnp.sin(angles)[..., None, :])


def time_embed(time_values, feature_count):
    halfway = feature_count // 2
    freq_index = jnp.arange(halfway).astype(jnp.float32)
    frequencies = jnp.exp(freq_index * (-math.log(10000.0) / halfway))
    angles = time_values.astype(jnp.float32)[..., None] * frequencies
    return jnp.concatenate([jnp.cos(angles), jnp.sin(angles)], axis=-1)


def slot_layout(segments, lengths):
    seg_range = jnp.arange(lengths.shape[-1], dtype=jnp.int32)
    membership = (segments[..., :, None] == seg_range).astype(jnp.float32)
    piece_sizes = jnp.sum(membership, axis=-2)
    piece_starts = jnp.cumsum(piece_sizes, axis=-1) - piece_sizes
    token_start = jnp.sum(membership * piece_starts[..., None, :], axis=-1)
    positions = jnp.arange(segments.shape[-1]).astype(jnp.float32) - token_start
    valid_limit = jnp.sum(membership * lengths.astype(jnp.float32)[..., None, :], axis=-1)
    validity = (positions < valid_limit).astype(jnp.float32)
    return (membership, positions, validity)


def block_order(matrix, seq_count, data_count):
    rows, cols = matrix.shape
    arranged = matrix.reshape(seq_count, rows // seq_count, data_count, cols // data_count)
    arranged = arranged.transpose(2, 0, 1, 3)
    return arranged.reshape(data_count * rows, cols // data_count)


def local(
    hidden_in,
    segment_ids,
    piece_lengths,
    time_index,
    first_gain,
    modulation_weight,
    modulation_bias,
    query_key_value_weight,
    attention_output_matrix,
    second_gain,
    widen_weight,
    expand_bias,
    narrow_weight,
    reduce_bias,
    cotangent,
):
    slot_count, own_rows, width = hidden_in.shape
    slot_rows = segment_ids.shape[1]
    head_count = HEADS
    head_dim = width // head_count
    score_scale = head_dim ** (-0.5)
    first_row = lax.axis_index("seq") * own_rows
    membership, positions, validity = slot_layout(segment_ids, piece_lengths)
    own_member = lax.dynamic_slice_in_dim(membership, first_row, own_rows, 1)
    own_pos = lax.dynamic_slice_in_dim(positions, first_row, own_rows, 1)
    own_valid = lax.dynamic_slice_in_dim(validity, first_row, own_rows, 1)
    own_segments = lax.dynamic_slice_in_dim(segment_ids, first_row, own_rows, 1)
    allowed = (own_segments[:, :, None] == segment_ids[:, None, :]) & (validity[:, None, :] > 0.5)
    condition = time_embed(time_index, modulation_weight.shape[0]).astype(jnp.bfloat16)
    modulation = (
        jnp.einsum("smc,cf->smf", condition, modulation_weight, preferred_element_type=jnp.float32)
        + modulation_bias
    )
    per_token = jnp.zeros((slot_count, own_rows, modulation.shape[-1]), jnp.float32)
    for segment in range(membership.shape[-1]):
        per_token = (
            per_token
            + own_member[:, :, segment : segment + 1] * modulation[:, segment : segment + 1, :]
        )
    shift_attn, scale_attn, gate_attn, shift_mlp, scale_mlp, gate_mlp = jnp.split(
        per_token, 6, axis=-1
    )
    residual = hidden_in.astype(jnp.float32)
    first_normed_tokens = norm_modulate(residual, first_gain, shift_attn, scale_attn).astype(
        jnp.bfloat16
    )
    triple = jnp.einsum(
        "map,pr->mar",
        first_normed_tokens,
        query_key_value_weight,
        preferred_element_type=jnp.float32,
    )
    query, key_raw, value_raw = jnp.split(triple, 3, axis=-1)
    four_dims = (slot_count, own_rows, head_count, head_dim)
    cosine, sine_part = rotary_tables(own_pos, head_dim)

    def turn(raw_values):
        return rotate(raw_values, cosine, sine_part)

    query_turned, turn_back = jax.vjp(turn, query.reshape(four_dims))
    query_rot = query_turned.astype(jnp.bfloat16)
    key_rot = (
        turn(key_raw.reshape(four_dims)).astype(jnp.bfloat16).reshape(slot_count, own_rows, width)
    )
    value_low = value_raw.astype(jnp.bfloat16)
    all_keys, all_values = (
        lax.all_gather(key_rot, "seq", axis=1, tiled=True),
        lax.all_gather(value_low, "seq", axis=1, tiled=True),
    )
    all_keys = all_keys.reshape(slot_count, slot_rows, head_count, head_dim)
    all_values = all_values.reshape(slot_count, slot_rows, head_count, head_dim)

    def attend(inputs):
        queries, keys, values, key_mask = inputs
        scores = (
            jnp.einsum("qhd,khd->hqk", queries, keys, preferred_element_type=jnp.float32)
            * score_scale
        )
        scores = jnp.where(key_mask[None], scores, negative)
        row_peak = jnp.max(scores, axis=-1, keepdims=True)
        exponent = jnp.exp(scores - row_peak)
        row_total = jnp.sum(exponent, axis=-1, keepdims=True)
        probability = exponent / row_total
        weighted = jnp.einsum(
            "hqk,khd->qhd",
            probability.astype(jnp.bfloat16),
            values,
            preferred_element_type=jnp.float32,
        )
        return (weighted, (row_peak + jnp.log(row_total))[..., 0])

    attended, log_total = lax.map(attend, (query_rot, all_keys, all_values, allowed))
    attention_result_narrow = attended.reshape(slot_count, own_rows, width).astype(jnp.bfloat16)
    projected = jnp.einsum(
        "rkn,nh->rkh",
        attention_result_narrow,
        attention_output_matrix,
        preferred_element_type=jnp.float32,
    )
    attn_branch = gate_attn * projected
    middle = residual + attn_branch
    second_normed_tokens = norm_modulate(middle, second_gain, shift_mlp, scale_mlp).astype(
        jnp.bfloat16
    )
    expanded = (
        jnp.einsum(
            "map,pr->mar", second_normed_tokens, widen_weight, preferred_element_type=jnp.float32
        )
        + expand_bias
    )
    gelu_activations = gelu_tanh(expanded).astype(jnp.bfloat16)
    reduced = (
        jnp.einsum(
            "jpb,bc->jpc", gelu_activations, narrow_weight, preferred_element_type=jnp.float32
        )
        + reduce_bias
    )
    mlp_branch = gate_mlp * reduced
    block_value = middle + mlp_branch
    block_out = block_value.astype(jnp.bfloat16)
    masked = own_valid[..., None]
    stat_terms = jnp.stack(
        [
            jnp.sum(masked * block_value * block_value),
            jnp.sum(masked * attn_branch * attn_branch),
            jnp.sum(masked * mlp_branch * mlp_branch),
            jnp.sum(own_valid),
        ]
    )
    grad_out = cotangent.astype(jnp.float32) * masked
    grad_gate_mlp = grad_out * reduced
    gradient_narrowed = (gate_mlp * grad_out).astype(jnp.bfloat16)
    reduce_weight_grad = jnp.einsum(
        "mhg,mhn->gn", gelu_activations, gradient_narrowed, preferred_element_type=jnp.float32
    )
    reduce_bias_grad = jnp.sum(gradient_narrowed.astype(jnp.float32), axis=(0, 1))
    grad_activated = jnp.einsum(
        "kav,cv->kac", gradient_narrowed, narrow_weight, preferred_element_type=jnp.float32
    )
    gradient_widened = jax.vjp(gelu_tanh, expanded)[1](grad_activated)[0].astype(jnp.bfloat16)
    expand_weight_grad = jnp.einsum(
        "cqe,cqr->er", second_normed_tokens, gradient_widened, preferred_element_type=jnp.float32
    )
    expand_bias_grad = jnp.sum(gradient_widened.astype(jnp.float32), axis=(0, 1))
    grad_normed_two = jnp.einsum(
        "yma,ja->ymj", gradient_widened, widen_weight, preferred_element_type=jnp.float32
    )
    second_back = jax.vjp(norm_modulate, middle, second_gain, shift_mlp, scale_mlp)[1]
    grad_middle_norm, second_gain_grad, grad_shift_mlp, grad_scale_mlp = second_back(
        grad_normed_two
    )
    grad_middle = grad_out + grad_middle_norm
    grad_gate_attn = grad_middle * projected
    gradient_attention_projected = (gate_attn * grad_middle).astype(jnp.bfloat16)
    output_weight_grad = jnp.einsum(
        "grm,gra->ma",
        attention_result_narrow,
        gradient_attention_projected,
        preferred_element_type=jnp.float32,
    )
    grad_attended = (
        jnp.einsum(
            "yzq,rq->yzr",
            gradient_attention_projected,
            attention_output_matrix,
            preferred_element_type=jnp.float32,
        )
        .astype(jnp.bfloat16)
        .reshape(four_dims)
    )

    def attend_back(inputs):
        queries, keys, values, key_mask, log_rows, grad_rows = inputs
        scores = (
            jnp.einsum("qhd,khd->hqk", queries, keys, preferred_element_type=jnp.float32)
            * score_scale
        )
        scores = jnp.where(key_mask[None], scores, negative)
        probability = jnp.exp(scores - log_rows[..., None])
        grad_values = jnp.einsum(
            "hqk,qhd->khd",
            probability.astype(jnp.bfloat16),
            grad_rows,
            preferred_element_type=jnp.float32,
        )
        grad_prob = jnp.einsum(
            "qhd,khd->hqk", grad_rows, values, preferred_element_type=jnp.float32
        )
        row_delta = jnp.sum(grad_prob * probability, axis=-1, keepdims=True)
        grad_scores = (probability * (grad_prob - row_delta)).astype(jnp.bfloat16)
        grad_queries = (
            jnp.einsum("hqk,khd->qhd", grad_scores, keys, preferred_element_type=jnp.float32)
            * score_scale
        )
        grad_keys = (
            jnp.einsum("hqk,qhd->khd", grad_scores, queries, preferred_element_type=jnp.float32)
            * score_scale
        )
        return (
            grad_queries,
            grad_keys.reshape(slot_rows, width),
            grad_values.reshape(slot_rows, width),
        )

    grad_query_rot, grad_key_part, grad_value_part = lax.map(
        attend_back, (query_rot, all_keys, all_values, allowed, log_total, grad_attended)
    )
    grad_key_rot, grad_value = (
        lax.psum_scatter(
            grad_key_part.astype(jnp.bfloat16), "seq", scatter_dimension=1, tiled=True
        ).astype(jnp.float32),
        lax.psum_scatter(
            grad_value_part.astype(jnp.bfloat16), "seq", scatter_dimension=1, tiled=True
        ).astype(jnp.float32),
    )
    grad_query = turn_back(grad_query_rot)[0].reshape(slot_count, own_rows, width)
    grad_key = turn_back(grad_key_rot.reshape(four_dims))[0].reshape(slot_count, own_rows, width)
    gradient_query_key_value = jnp.concatenate([grad_query, grad_key, grad_value], axis=-1).astype(
        jnp.bfloat16
    )
    triple_weight_grad = jnp.einsum(
        "cqe,cqr->er",
        first_normed_tokens,
        gradient_query_key_value,
        preferred_element_type=jnp.float32,
    )
    grad_normed_one = jnp.einsum(
        "yma,ja->ymj",
        gradient_query_key_value,
        query_key_value_weight,
        preferred_element_type=jnp.float32,
    )
    first_back = jax.vjp(norm_modulate, residual, first_gain, shift_attn, scale_attn)[1]
    grad_residual, first_gain_grad, grad_shift_attn, grad_scale_attn = first_back(grad_normed_one)
    input_grad = (grad_middle + grad_residual).astype(jnp.bfloat16)
    grad_tokens = jnp.concatenate(
        [
            grad_shift_attn,
            grad_scale_attn,
            grad_gate_attn,
            grad_shift_mlp,
            grad_scale_mlp,
            grad_gate_mlp,
        ],
        axis=-1,
    )
    grad_modulation = jnp.einsum(
        "slm,slf->smf",
        own_member,
        grad_tokens,
        precision=highest,
        preferred_element_type=jnp.float32,
    )
    modulation_weight_grad = jnp.einsum(
        "smc,smf->cf",
        condition.astype(jnp.float32),
        grad_modulation,
        precision=highest,
        preferred_element_type=jnp.float32,
    )
    modulation_bias_grad = jnp.sum(grad_modulation, axis=(0, 1))
    vectors = [
        first_gain_grad,
        modulation_bias_grad,
        second_gain_grad,
        expand_bias_grad,
        reduce_bias_grad,
        stat_terms,
    ]
    flat_small = jnp.concatenate(vectors)
    summed_small = lax.psum(flat_small, ("dp", "seq"))
    small_results = []
    cursor = 0
    for vector in vectors:
        small_results.append(summed_small[cursor : cursor + vector.shape[0]])
        cursor = cursor + vector.shape[0]
    seq_count = lax.axis_size("seq")
    data_count = lax.axis_size("dp")
    matrix_parts = (
        lax.psum_scatter(
            block_order(modulation_weight_grad, seq_count, data_count),
            ("dp", "seq"),
            scatter_dimension=0,
            tiled=True,
        ),
        lax.psum_scatter(
            block_order(triple_weight_grad, seq_count, data_count),
            ("dp", "seq"),
            scatter_dimension=0,
            tiled=True,
        ),
        lax.psum_scatter(
            block_order(output_weight_grad, seq_count, data_count),
            ("dp", "seq"),
            scatter_dimension=0,
            tiled=True,
        ),
        lax.psum_scatter(
            block_order(expand_weight_grad, seq_count, data_count),
            ("dp", "seq"),
            scatter_dimension=0,
            tiled=True,
        ),
        lax.psum_scatter(
            block_order(reduce_weight_grad, seq_count, data_count),
            ("dp", "seq"),
            scatter_dimension=0,
            tiled=True,
        ),
    )
    totals = small_results[5]
    masked_rms = jnp.sqrt(totals[:3] / (totals[3] * width))
    return (
        block_out,
        input_grad,
        small_results[0],
        matrix_parts[0],
        small_results[1],
        matrix_parts[1],
        matrix_parts[2],
        small_results[2],
        matrix_parts[3],
        small_results[3],
        matrix_parts[4],
        small_results[4],
        masked_rms,
    )


def solution(mesh):
    in_specs = (
        P("dp", "seq", None),
        P("dp", None),
        P("dp", None),
        P("dp", None),
        P(),
        P(),
        P(),
        P(),
        P(),
        P(),
        P(),
        P(),
        P(),
        P(),
        P("dp", "seq", None),
    )
    out_specs = (
        P("dp", "seq", None),
        P("dp", "seq", None),
        P(),
        P("seq", "dp"),
        P(),
        P("seq", "dp"),
        P("seq", "dp"),
        P(),
        P("seq", "dp"),
        P(),
        P("seq", "dp"),
        P(),
        P(),
    )
    return jax.shard_map(local, mesh=mesh, in_specs=in_specs, out_specs=out_specs, check_vma=False)
```

profile of v0, /device:TPU:0, one launch (start us, length us, event | category | flops | bytes accessed | tf_op | source)
XLA Modules:
  0.0 905.5 jit_solution(2485126166303341673)
XLA Ops:
  26.8 3.1 copy.74
  29.8 2.3 mul.818
  32.1 3.0 copy.71
  36.2 6.6 multiply_add_fusion.2
  43.4 2.0 convolution_bitcast_fusion.1
  46.7 2.1 copy-done.20
  50.2 3.0 copy.72
  56.2 3.0 copy.73
  59.2 5.1 add_convert_fusion.1
  64.3 2.4 split.98
  68.1 3.1 copy.69
  75.4 18.9 %all-gather.5.cloned.1.call-done = bf16[1,1024,768]{2,1,0:T(8,128)(2,1)} async-done(((bf16[1,512,768]{2,1,0:T(8,128)(2,1)}), bf16[1,1024,768]{2,1,0:T(8,128)(2,1)}) %all-gather.5.cloned.1.call-update) | async-done | bytes 1572880 | tf_op jit(solution)/shard_map/all_gather | solution.py:135
  94.4 2.7 copy.75
  97.0 14.8 %fusion.8 = (f32[12,512]{1,0:T(8,128)S(1)}, f32[12,512,1024]{2,1,0:T(8,128)}) fusion(pred[512,1024]{1,0:T(8,128)(4,1)} %compare_and_fusion, bf16[512,12,64]{0,2,1:T(8,128)(2,1)} %fusion.57, bf16[1024,12,64]{0,2,1:T(8,128)(2,1)} %bitcast.275), kind=kOutput, calls=%fused_computation.20 | convolution fusion | flops 824174592 | bytes 28073984 | tf_op jit(solution)/shard_map/while/body/eval_jaxpr/qhd,khd->hqk/dot_general | solution.py:144
  111.8 11.8 %fusion = f32[12,512]{1,0:T(8,128)S(1)} fusion(f32[12,512]{1,0:T(8,128)S(1)} %get-tuple-element.132, f32[12,512,1024]{2,1,0:T(8,128)} %get-tuple-element.133, pred[512,1024]{1,0:T(8,128)(4,1)S(1)} %copy-done.15), kind=kLoop, calls=%fused_computation.6 | loop fusion | flops 25159680 | bytes 25739264 | tf_op jit(solution)/shard_map/while/body/eval_jaxpr/reduce_sum | solution.py:150
  124.9 2.6 copy.68
  127.5 13.2 %fusion.64 = bf16[12,64,512]{2,1,0:T(8,128)(2,1)S(1)} fusion(bf16[1024,12,64]{0,2,1:T(8,128)(2,1)} %bitcast.280, f32[12,512]{1,0:T(8,128)} %copy-done.39, f32[12,512]{1,0:T(8,128)} %copy-done.38, f32[12,512,1024]{2,1,0:T(8,128)} %get-tuple-element.133, pred[512,1024]{1,0:T(8,128)(4,1)} %compare_and_fusion), kind=kOutput, calls=%fused_computation.130 | convolution fusion | flops 837156864 | bytes 28098560 | tf_op jit(solution)/shard_map/while/body/eval_jaxpr/hqk,khd->qhd/dot_general | solution.py:152
  140.8 2.7 fusion.102
  145.2 2.6 fusion.69
  148.0 5.1 fusion.30
  153.1 12.1 %convert_reduce_fusion = (f32[3072]{0:T(1024)}, bf16[512,3072]{1,0:T(8,128)(2,1)}, f32[512,3072]{1,0:T(8,128)}) fusion(f32[512,3072]{1,0:T(8,128)S(1)} %fusion.69, f32[3072]{0:T(1024)S(1)} %copy-done.59, bf16[3072,768]{1,0:T(8,128)(2,1)} %param.27, bf16[1,512,768]{2,1,0:T(8,128)(2,1)S(1)} %get-tuple-element.85), kind=kOutput, calls=%fused_computation.46 | convolution fusion | flops 2458383360 | bytes 21258240 | tf_op jit(solution)/shard_map/kav,cv->kac/dot_general | solution.py:205
  165.2 7.6 multiply_reduce_fusion.1
  176.0 1.7 convolution_convert_fusion
  177.7 2.3 copy.76
  180.0 18.8 %multiply_reduce_fusion = (f32[12,512]{1,0:T(8,128)}, f32[12,512,1024]{2,1,0:T(8,128)}) fusion(f32[12,512]{1,0:T(8,128)} %log_add_fusion, f32[12,512,1024]{2,1,0:T(8,128)} %get-tuple-element.133, pred[512,1024]{1,0:T(8,128)(4,1)} %compare_and_fusion, bf16[512,12,64]{0,2,1:T(8,128)(2,1)} %bitcast.302, bf16[1024,12,64]{0,2,1:T(8,128)(2,1)} %bitcast.281), kind=kOutput, calls=%fused_computation.1 | convolution fusion | flops 836757504 | bytes 53264384 | tf_op jit(solution)/shard_map/while/body/eval_jaxpr/qhd,khd->hqk/dot_general | solution.py:254
  198.8 17.6 %multiply_convert_fusion = bf16[12,512,1024]{2,1,0:T(8,128)(2,1)S(1)} fusion(f32[12,512,1024]{2,1,0:T(8,128)} %get-tuple-element.138, f32[12,512]{1,0:T(8,128)} %get-tuple-element.137, f32[12,512]{1,0:T(8,128)} %log_add_fusion, f32[12,512,1024]{2,1,0:T(8,128)} %get-tuple-element.133, pred[512,1024]{1,0:T(8,128)(4,1)} %compare_and_fusion), kind=kLoop, calls=%fused_computation | loop fusion | flops 37748736 | bytes 63488000 | tf_op jit(solution)/shard_map/while/body/eval_jaxpr/convert_element_type | solution.py:258
  216.4 4.1 multiply_convert_fusion.2
  221.5 13.7 %fusion.38 = bf16[12,64,1024]{2,1,0:T(8,128)(2,1)} fusion(bf16[512,12,64]{0,2,1:T(8,128)(2,1)} %bitcast.303, f32[12,512]{1,0:T(8,128)} %log_add_fusion, f32[12,512,1024]{2,1,0:T(8,128)} %get-tuple-element.133, pred[512,1024]{1,0:T(8,128)(4,1)} %compare_and_fusion), kind=kOutput, calls=%fused_computation.77 | convolution fusion | flops 831258624 | bytes 28073984 | tf_op jit(solution)/shard_map/while/body/eval_jaxpr/hqk,qhd->khd/dot_general | solution.py:248
  238.0 2.3 copy.82
  240.3 2.2 convolution_bitcast_fusion.5
  242.5 3.3 copy.83
  245.7 4.4 reshape.1485
  250.1 9.0 fusion.107
  262.0 3.2 fusion.59
  268.0 8.4 reduce-scatter.10.cloned.1.call-done
  276.3 3.7 bitcast_dynamic-update-slice_fusion
  280.1 2.4 fusion.51
  283.9 2.0 fusion.63
  289.9 4.4 fusion.106
  294.3 1.7 dot_general.140
  296.0 2.4 convolution_bitcast_fusion.4
  298.4 1.9 copy.79
  300.3 2.3 copy.98
  302.7 11.0 %multiply_convert_fusion.1 = (bf16[3072,512]{0,1:T(8,128)(2,1)}, bf16[3072,512]{0,1:T(8,128)(2,1)}) fusion(f32[512,3072]{1,0:T(8,128)} %copy-done.8, f32[3072]{0:T(1024)S(1)} %copy-done.60, f32[512,3072]{1,0:T(8,128)} %get-tuple-element.135), kind=kLoop, calls=%fused_computation.45 | loop fusion | flops 42467328 | bytes 18886656 | tf_op jit(solution)/shard_map/convert_element_type | solution.py:179
  313.6 4.8 copy.84
  318.4 4.8 convolution_bitcast_fusion.2
  323.2 12.7 %copy.86 = f32[16,2,384,192]{2,1,0,3:T(2,128)} copy(f32[16,2,384,192]{2,3,0,1:T(8,128)S(1)} %convolution_bitcast_fusion.2) | data formatting | bytes 18874368 | tf_op jit(solution)/shard_map/transpose | solution.py:64
  336.0 12.5 %reshape.1486 = f32[12288,192]{0,1:T(8,128)} reshape(f32[16,2,384,192]{2,1,0,3:T(2,128)} %copy.86) | data formatting | bytes 18874368 | tf_op jit(solution)/shard_map/reshape | solution.py:65
  348.6 2.3 copy.87
  350.9 4.8 copy.99
  355.7 4.7 convolution_bitcast_fusion
  360.5 11.1 %copy.89 = f32[16,2,1536,48]{2,1,0,3:T(2,128)} copy(f32[16,2,1536,48]{2,3,0,1:T(8,128)S(1)} %convolution_bitcast_fusion) | data formatting | bytes 18874368 | tf_op jit(solution)/shard_map/transpose | solution.py:64
  371.6 12.2 %reshape.1487 = f32[49152,48]{0,1:T(8,128)} reshape(f32[16,2,1536,48]{2,1,0,3:T(2,128)} %copy.89) | data formatting | bytes 18874368 | tf_op jit(solution)/shard_map/reshape | solution.py:65
  383.9 2.3 copy.97
  386.2 1.8 pad_maximum_fusion
  388.1 4.5 convolution_bitcast_fusion.3
  392.5 11.4 %copy.81 = f32[16,2,384,144]{2,1,0,3:T(2,128)} copy(f32[16,2,384,144]{2,3,0,1:T(8,128)} %convolution_bitcast_fusion.3) | data formatting | bytes 14155776 | tf_op jit(solution)/shard_map/transpose | solution.py:64
  403.9 9.8 %reshape.1484 = f32[12288,144]{0,1:T(8,128)} reshape(f32[16,2,384,144]{2,1,0,3:T(2,128)} %copy.81) | data formatting | bytes 14155776 | tf_op jit(solution)/shard_map/reshape | solution.py:65
  414.5 3.9 concatenate.72
  418.4 40.4 %psum.7 = f32[9988]{0:T(1024)} all-reduce(f32[9988]{0:T(1024)} %concatenate.72), channel_id=1, replica_groups=mesh['dp'=16,'seq'=2] {'dp','seq'}, use_global_device_ids=true, to_apply=%region_26.27 | all-reduce | flops 9988 | bytes 79904 | tf_op jit(solution)/shard_map/psum | solution.py:339
  465.9 22.6 %reduce-scatter.12.cloned.1.call-done = f32[64,288]{1,0:T(8,128)} async-done(((f32[2048,288]{1,0:T(8,128)}), f32[64,288]{1,0:T(8,128)}) %reduce-scatter.12.cloned.1.call-update) | async-done | bytes 73744 | tf_op jit(solution)/shard_map/reduce_scatter | solution.py:348
  488.5 141.9 %reduce-scatter.18.cloned.1.call-done = f32[384,192]{0,1:T(8,128)} async-done(((f32[12288,192]{0,1:T(8,128)}), f32[384,192]{0,1:T(8,128)}) %reduce-scatter.18.cloned.1.call-update) | async-done | bytes 294928 | tf_op jit(solution)/shard_map/reduce_scatter | solution.py:366
  630.4 143.0 %reduce-scatter.20.cloned.1.call-done = f32[1536,48]{0,1:T(8,128)} async-done(((f32[49152,48]{0,1:T(8,128)}), f32[1536,48]{0,1:T(8,128)}) %reduce-scatter.20.cloned.1.call-update) | async-done | bytes 294928 | tf_op jit(solution)/shard_map/reduce_scatter | solution.py:372
  773.4 125.4 %reduce-scatter.14.cloned.1.call-done = f32[384,144]{0,1:T(8,128)} async-done(((f32[12288,144]{0,1:T(8,128)}), f32[384,144]{0,1:T(8,128)}) %reduce-scatter.14.cloned.1.call-update) | async-done | bytes 221200 | tf_op jit(solution)/shard_map/reduce_scatter | solution.py:354
  (227 shorter events, 60.7 us)
Async XLA Ops:
  7.2 36.2 %copy-start = (bf16[768,2304]{1,0:T(8,128)(2,1)S(1)}, bf16[768,2304]{1,0:T(8,128)(2,1)}, u32[]{:S(2)}) copy-start(bf16[768,2304]{1,0:T(8,128)(2,1)} %param.22) | copy-start | bytes 10616836
  7.2 87.2 %all-gather.5.cloned.1.call-start = ((), (), s32[]{:S(2)}) async-start(), calls=%async_computation.8 | async-start | bytes 2359296 | tf_op jit(solution)/shard_map/all_gather | solution.py:135
  11.4 31.4 %copy-start.41 = (f32[512]{0:T(512)}, f32[512]{0:T(512)S(1)}, u32[]{:S(2)}) copy-start(f32[512]{0:T(512)S(1)} %broadcast_multiply_fusion.4) | copy-start | bytes 6148
  13.5 29.3 %copy-start.45 = (f32[512]{0:T(512)}, f32[512]{0:T(512)S(1)}, u32[]{:S(2)}) copy-start(f32[512]{0:T(512)S(1)} %fusion.84) | copy-start | bytes 6148
  18.6 3.2 copy-start.51
  36.2 6.6 copy-start.5
  36.2 6.6 copy-start.43
  42.9 3.6 copy-start.2
  43.4 3.3 copy-start.23
  46.7 2.1 copy-start.20
  64.3 2.7 copy-start.40
  64.3 3.3 copy-start.48
  64.3 60.6 %all-gather.3.cloned.1.call-start = ((), (), s32[]{:S(2)}) async-start(), calls=%async_computation.7 | async-start | bytes 2359296 | tf_op jit(solution)/shard_map/all_gather | solution.py:136
  66.7 198.4 %reduce-scatter.8.cloned.1.call-start = ((), (), s32[]{:S(2)}) async-start(), calls=%async_computation.9 | async-start | bytes 2359296 | tf_op jit(solution)/shard_map/reduce_scatter | solution.py:277
  68.1 4.7 copy-start.61
  68.1 4.7 copy-start.62
  71.2 2.9 copy-start.9
  71.2 2.9 copy-start.28
  71.2 2.9 copy-start.31
  97.0 14.8 %copy-start.15 = (pred[512,1024]{1,0:T(8,128)(4,1)S(1)}, pred[512,1024]{1,0:T(8,128)(4,1)}, u32[]{:S(2)}) copy-start(pred[512,1024]{1,0:T(8,128)(4,1)} %compare_and_fusion) | copy-start | bytes 1572868
  111.8 11.8 %copy-start.38 = (f32[12,512]{1,0:T(8,128)}, f32[12,512]{1,0:T(8,128)S(1)}, u32[]{:S(2)}) copy-start(f32[12,512]{1,0:T(8,128)S(1)} %get-tuple-element.132) | copy-start | bytes 73732
  127.5 16.3 %slice-start = ((s8[9437184]{0:T(1024)(128)(4,1)}), s8[4194304]{0:T(1024)(128)(4,1)S(1)}, s32[]{:S(2)}) async-start(s8[9437184]{0:T(1024)(128)(4,1)} %bitcast.271), calls=%async_computation.16 | async-start | bytes 8388608
  127.5 13.2 %copy-start.6 = (bf16[1,512,768]{2,1,0:T(8,128)(2,1)S(1)}, bf16[1,512,768]{2,1,0:T(8,128)(2,1)}, u32[]{:S(2)}) copy-start(bf16[1,512,768]{2,1,0:T(8,128)(2,1)} %param.15) | copy-start | bytes 2359300
  127.5 13.2 %copy-start.34 = (bf16[768,768]{1,0:T(8,128)(2,1)S(1)}, bf16[768,768]{1,0:T(8,128)(2,1)}, u32[]{:S(2)}) copy-start(bf16[768,768]{1,0:T(8,128)(2,1)} %param.23) | copy-start | bytes 3538948
  127.5 16.3 %slice-start.1 = ((s8[9437184]{0:T(1024)(128)(4,1)}), s8[4194304]{0:T(1024)(128)(4,1)S(1)}, s32[]{:S(2)}) async-start(s8[9437184]{0:T(1024)(128)(4,1)} %bitcast.271), calls=%async_computation.17 | async-start | bytes 8388608
  127.5 16.3 %slice-start.2 = ((s8[9437184]{0:T(1024)(128)(4,1)}), s8[1048576]{0:T(1024)(128)(4,1)S(1)}, s32[]{:S(2)}) async-start(s8[9437184]{0:T(1024)(128)(4,1)} %bitcast.271), calls=%async_computation.18 | async-start | bytes 2097152
  140.7 2.7 copy-start.26
  140.7 3.1 copy-start.16
  140.7 3.1 copy-start.47
  140.7 4.4 slice-start.3
  143.4 21.8 %copy-start.21 = (f32[512,768]{1,0:T(8,128)}, f32[512,768]{1,0:T(8,128)S(1)}, u32[]{:S(2)}) copy-start(f32[512,768]{1,0:T(8,128)S(1)} %get-tuple-element.134) | copy-start | bytes 4718596
  143.4 29.3 %copy-start.3 = (f32[1,512,768]{2,1,0:T(8,128)}, f32[1,512,768]{2,1,0:T(8,128)S(1)}, u32[]{:S(2)}) copy-start(f32[1,512,768]{2,1,0:T(8,128)S(1)} %get-tuple-element.94) | copy-start | bytes 4718596
  143.5 1.7 slice-start.4
  143.8 4.0 slice-start.5
  145.1 2.7 copy-start.19
  145.1 8.0 copy-start.24
  145.2 2.7 copy-start.59
  145.2 2.8 slice-start.6
  148.0 5.1 copy-start.8
  153.1 12.1 %copy-start.64 = (f32[768]{0:T(1024)S(1)}, f32[768]{0:T(1024)}, u32[]{:S(2)}) copy-start(f32[768]{0:T(1024)} %param.28) | copy-start | bytes 9220
  173.9 2.1 copy-start.35
  198.8 17.6 %copy-start.18 = (bf16[512,12,64]{0,2,1:T(8,128)(2,1)S(1)}, bf16[512,12,64]{0,2,1:T(8,128)(2,1)}, u32[]{:S(2)}) copy-start(bf16[512,12,64]{0,2,1:T(8,128)(2,1)} %fusion.57) | copy-start | bytes 2359300
  216.4 5.1 copy-start.1
  221.5 54.8 %reduce-scatter.10.cloned.1.call-start = ((), (), s32[]{:S(2)}) async-start(), calls=%async_computation.10 | async-start | bytes 2359296 | tf_op jit(solution)/shard_map/reduce_scatter | solution.py:280
  235.3 230.6 %reduce-scatter.16.cloned.1.call-start = ((), (), s32[]{:S(2)}) async-start(), calls=%async_computation.13 | async-start | bytes 2433024 | tf_op jit(solution)/shard_map/reduce_scatter | solution.py:360
  250.1 10.3 %copy-start.37 = (f32[512,64]{0,1:T(8,128)S(1)}, f32[512,64]{0,1:T(8,128)}, u32[]{:S(2)}) copy-start(f32[512,64]{0,1:T(8,128)} %get-tuple-element.114) | copy-start | bytes 393220
  261.9 226.6 %reduce-scatter.12.cloned.1.call-start = ((), (), s32[]{:S(2)}) async-start(), calls=%async_computation.11 | async-start | bytes 3244032 | tf_op jit(solution)/shard_map/reduce_scatter | solution.py:348
  276.3 3.7 copy-start.7
  276.3 3.7 copy-start.42
  276.3 3.8 copy-start.44
  276.3 3.8 copy-start.46
  280.1 2.4 copy-start.50
  280.1 3.8 copy-start.13
  280.1 3.8 copy-start.17
  280.1 3.8 copy-start.22
  280.1 3.8 copy-start.55
  283.9 2.0 copy-start.11
  285.9 1.9 copy-start.33
  289.9 6.1 copy-start.58
  300.3 2.4 copy-start.60
  300.3 330.1 %reduce-scatter.18.cloned.1.call-start = ((), (), s32[]{:S(2)}) async-start(), calls=%async_computation.14 | async-start | bytes 9732096 | tf_op jit(solution)/shard_map/reduce_scatter | solution.py:366
  348.5 424.8 %reduce-scatter.20.cloned.1.call-start = ((), (), s32[]{:S(2)}) async-start(), calls=%async_computation.15 | async-start | bytes 9732096 | tf_op jit(solution)/shard_map/reduce_scatter | solution.py:372
  383.8 514.9 %reduce-scatter.14.cloned.1.call-start = ((), (), s32[]{:S(2)}) async-start(), calls=%async_computation.12 | async-start | bytes 7299072 | tf_op jit(solution)/shard_map/reduce_scatter | solution.py:354
  386.2 1.8 copy-start.36
  (18 other events, 19.0 us)
Sparse Core Ops, SparseCore 0:
  64.4 29.8 all-gather.4
  96.5 27.2 all-gather.2
  221.6 26.3 reduce-scatter.7
  250.2 26.0 reduce-scatter.9
  282.0 99.0 reduce-scatter.15
  387.9 100.5 reduce-scatter.11
  496.0 134.3 reduce-scatter.17
  636.9 136.4 reduce-scatter.19
  780.6 118.1 reduce-scatter.13
where the time goes:
time: 914 us; the launch traced here: 906 us
  waiting for transfers between devices  460 us (50%)
  local copies, waits for them, and re-layouts  157 us (17%)
  matrix products  136 us (15%)
  other arithmetic  96.3 us (11%)
  blocking collectives  40.4 us (4%)
  between operations  15.5 us (2%)
    reduce_scatter x1, waiting for transfers between devices, local(): lax.psum_scatter(block_order(reduce_weight_grad, seq_count, data_count),...  143 us
    reduce_scatter x1, waiting for transfers between devices, local(): lax.psum_scatter(block_order(expand_weight_grad, seq_count, data_count),...  142 us
    reduce_scatter x1, waiting for transfers between devices, local(): lax.psum_scatter(block_order(triple_weight_grad, seq_count, data_count),...  125 us
    psum x1, blocking collectives, local(): summed_small = lax.psum(flat_small, ('dp', 'seq'))  40.4 us
    transpose x5, local copies, waits for them, and re-layouts, block_order(): arranged = arranged.transpose(2, 0, 1, 3)  40.4 us
    reshape x4, local copies, waits for them, and re-layouts, block_order(): return arranged.reshape(data_count * rows, cols // data_count)  39 us
    reduce_scatter x1, waiting for transfers between devices, local(): lax.psum_scatter(block_order(modulation_weight_grad, seq_count, data_coun...  22.6 us
    all_gather x1, waiting for transfers between devices, local(): lax.all_gather(key_rot, 'seq', axis=1, tiled=True)  18.9 us
  transfers between devices with their start and end apart: 9, of which 6 were waited for; matrix products, arithmetic and copies ran while one was open for 25% of the time, Pallas kernels for 0%

commit v1 on v0

--- a/solution.py
+++ b/solution.py
@@ -336,7 +336,7 @@
         stat_terms,
     ]
     flat_small = jnp.concatenate(vectors)
-    summed_small = lax.psum(flat_small, ("dp", "seq"))
+    summed_small = lax.psum(lax.psum(flat_small, "seq"), "dp")
     small_results = []
     cursor = 0
     for vector in vectors:

time: 914 us -> 914 us (level)
  blocking collectives: 40.4 us -> 69.4 us
  waiting for transfers between devices: 460 us -> 432 us
    psum x1 -> x2, blocking collectives: 40.4 us -> 69.4 us  [local(): summed_small = lax.psum(lax.psum(flat_small, 'seq'), 'dp')]
    reduce_scatter x1, waiting for transfers between devices: 22.6 us -> 0.01 us  [local(): lax.psum_scatter(block_order(modulation_weight_grad, seq_count, data_coun...]
  transfers between devices with their start and end apart: 9 -> 9, of which waited for: 6 -> 5; matrix products, arithmetic and copies ran while one was open for 25% -> 25% of each run, Pallas kernels for 0% -> 0%
where the time goes in v1:
time: 914 us; the launch traced here: 905 us
  waiting for transfers between devices  432 us (47%)
  local copies, waits for them, and re-layouts  157 us (17%)
  matrix products  135 us (15%)
  other arithmetic  96.3 us (11%)
  blocking collectives  69.4 us (8%)
  between operations  15.5 us (2%)
    reduce_scatter x1, waiting for transfers between devices, local(): lax.psum_scatter(block_order(reduce_weight_grad, seq_count, data_count),...  143 us
    reduce_scatter x1, waiting for transfers between devices, local(): lax.psum_scatter(block_order(expand_weight_grad, seq_count, data_count),...  136 us
    reduce_scatter x1, waiting for transfers between devices, local(): lax.psum_scatter(block_order(triple_weight_grad, seq_count, data_count),...  125 us
    psum x2, blocking collectives, local(): summed_small = lax.psum(lax.psum(flat_small, 'seq'), 'dp')  69.4 us
    transpose x5, local copies, waits for them, and re-layouts, block_order(): arranged = arranged.transpose(2, 0, 1, 3)  40.4 us
    reshape x4, local copies, waits for them, and re-layouts, block_order(): return arranged.reshape(data_count * rows, cols // data_count)  38.9 us
    all_gather x1, waiting for transfers between devices, local(): lax.all_gather(key_rot, 'seq', axis=1, tiled=True)  18.9 us
    dot_general x1, matrix products, attend_back(): jnp.einsum('qhd,khd->hqk', grad_rows, values, preferred_element_type=jnp....  18.8 us
  transfers between devices with their start and end apart: 9, of which 5 were waited for; matrix products, arithmetic and copies ran while one was open for 25% of the time, Pallas kernels for 0%

profile of v1, /device:TPU:0, one launch (start us, length us, event | category | flops | bytes accessed | tf_op | source)
XLA Modules:
  0.0 905.4 jit_solution(8465253501353433925)
XLA Ops:
  26.7 3.0 copy.74
  29.8 2.2 mul.818
  32.0 3.0 copy.71
  36.2 6.6 multiply_add_fusion.2
  43.3 2.0 convolution_bitcast_fusion.1
  46.6 2.1 copy-done.20
  50.1 3.0 copy.72
  56.1 3.1 copy.73
  59.2 5.1 add_convert_fusion.1
  64.3 2.4 split.98
  68.1 3.1 copy.69
  75.4 18.9 %all-gather.5.cloned.1.call-done = bf16[1,1024,768]{2,1,0:T(8,128)(2,1)} async-done(((bf16[1,512,768]{2,1,0:T(8,128)(2,1)}), bf16[1,1024,768]{2,1,0:T(8,128)(2,1)}) %all-gather.5.cloned.1.call-update) | async-done | bytes 1572880 | tf_op jit(solution)/shard_map/all_gather | solution.py:135
  94.3 2.7 copy.75
  97.0 14.8 %fusion.8 = (f32[12,512]{1,0:T(8,128)S(1)}, f32[12,512,1024]{2,1,0:T(8,128)}) fusion(pred[512,1024]{1,0:T(8,128)(4,1)} %compare_and_fusion, bf16[512,12,64]{0,2,1:T(8,128)(2,1)} %fusion.57, bf16[1024,12,64]{0,2,1:T(8,128)(2,1)} %bitcast.275), kind=kOutput, calls=%fused_computation.20 | convolution fusion | flops 824174592 | bytes 28073984 | tf_op jit(solution)/shard_map/while/body/eval_jaxpr/qhd,khd->hqk/dot_general | solution.py:144
  111.8 11.8 %fusion = f32[12,512]{1,0:T(8,128)S(1)} fusion(f32[12,512]{1,0:T(8,128)S(1)} %get-tuple-element.132, f32[12,512,1024]{2,1,0:T(8,128)} %get-tuple-element.133, pred[512,1024]{1,0:T(8,128)(4,1)S(1)} %copy-done.15), kind=kLoop, calls=%fused_computation.6 | loop fusion | flops 25159680 | bytes 25739264 | tf_op jit(solution)/shard_map/while/body/eval_jaxpr/reduce_sum | solution.py:150
  124.8 2.6 copy.68
  127.4 13.2 %fusion.64 = bf16[12,64,512]{2,1,0:T(8,128)(2,1)S(1)} fusion(bf16[1024,12,64]{0,2,1:T(8,128)(2,1)} %bitcast.280, f32[12,512]{1,0:T(8,128)} %copy-done.39, f32[12,512]{1,0:T(8,128)} %copy-done.38, f32[12,512,1024]{2,1,0:T(8,128)} %get-tuple-element.133, pred[512,1024]{1,0:T(8,128)(4,1)} %compare_and_fusion), kind=kOutput, calls=%fused_computation.130 | convolution fusion | flops 837156864 | bytes 28098560 | tf_op jit(solution)/shard_map/while/body/eval_jaxpr/hqk,khd->qhd/dot_general | solution.py:152
  140.7 2.7 fusion.102
  145.1 2.6 fusion.69
  147.9 5.1 fusion.30
  153.0 12.1 %convert_reduce_fusion = (f32[3072]{0:T(1024)}, bf16[512,3072]{1,0:T(8,128)(2,1)}, f32[512,3072]{1,0:T(8,128)}) fusion(f32[512,3072]{1,0:T(8,128)S(1)} %fusion.69, f32[3072]{0:T(1024)S(1)} %copy-done.59, bf16[3072,768]{1,0:T(8,128)(2,1)} %param.27, bf16[1,512,768]{2,1,0:T(8,128)(2,1)S(1)} %get-tuple-element.85), kind=kOutput, calls=%fused_computation.46 | convolution fusion | flops 2458383360 | bytes 21258240 | tf_op jit(solution)/shard_map/kav,cv->kac/dot_general | solution.py:205
  165.1 7.5 multiply_reduce_fusion.1
  175.9 1.7 convolution_convert_fusion
  177.6 2.3 copy.76
  179.9 18.8 %multiply_reduce_fusion = (f32[12,512]{1,0:T(8,128)}, f32[12,512,1024]{2,1,0:T(8,128)}) fusion(f32[12,512]{1,0:T(8,128)} %log_add_fusion, f32[12,512,1024]{2,1,0:T(8,128)} %get-tuple-element.133, pred[512,1024]{1,0:T(8,128)(4,1)} %compare_and_fusion, bf16[512,12,64]{0,2,1:T(8,128)(2,1)} %bitcast.302, bf16[1024,12,64]{0,2,1:T(8,128)(2,1)} %bitcast.281), kind=kOutput, calls=%fused_computation.1 | convolution fusion | flops 836757504 | bytes 53264384 | tf_op jit(solution)/shard_map/while/body/eval_jaxpr/qhd,khd->hqk/dot_general | solution.py:254
  198.7 17.6 %multiply_convert_fusion = bf16[12,512,1024]{2,1,0:T(8,128)(2,1)S(1)} fusion(f32[12,512,1024]{2,1,0:T(8,128)} %get-tuple-element.138, f32[12,512]{1,0:T(8,128)} %get-tuple-element.137, f32[12,512]{1,0:T(8,128)} %log_add_fusion, f32[12,512,1024]{2,1,0:T(8,128)} %get-tuple-element.133, pred[512,1024]{1,0:T(8,128)(4,1)} %compare_and_fusion), kind=kLoop, calls=%fused_computation | loop fusion | flops 37748736 | bytes 63488000 | tf_op jit(solution)/shard_map/while/body/eval_jaxpr/convert_element_type | solution.py:258
  216.3 4.1 multiply_convert_fusion.2
  221.4 13.7 %fusion.38 = bf16[12,64,1024]{2,1,0:T(8,128)(2,1)} fusion(bf16[512,12,64]{0,2,1:T(8,128)(2,1)} %bitcast.303, f32[12,512]{1,0:T(8,128)} %log_add_fusion, f32[12,512,1024]{2,1,0:T(8,128)} %get-tuple-element.133, pred[512,1024]{1,0:T(8,128)(4,1)} %compare_and_fusion), kind=kOutput, calls=%fused_computation.77 | convolution fusion | flops 831258624 | bytes 28073984 | tf_op jit(solution)/shard_map/while/body/eval_jaxpr/hqk,qhd->khd/dot_general | solution.py:248
  237.9 2.3 copy.82
  240.1 2.2 convolution_bitcast_fusion.5
  242.3 3.3 copy.83
  245.6 4.4 reshape.1485
  250.0 9.0 fusion.107
  261.8 3.2 fusion.59
  267.8 8.4 reduce-scatter.10.cloned.1.call-done
  276.2 3.7 bitcast_dynamic-update-slice_fusion
  280.0 2.4 fusion.51
  283.8 2.0 fusion.63
  289.8 4.4 fusion.106
  294.1 1.7 dot_general.140
  295.9 2.4 convolution_bitcast_fusion.4
  298.2 1.9 copy.79
  300.2 2.3 copy.98
  302.5 11.0 %multiply_convert_fusion.1 = (bf16[3072,512]{0,1:T(8,128)(2,1)}, bf16[3072,512]{0,1:T(8,128)(2,1)}) fusion(f32[512,3072]{1,0:T(8,128)} %copy-done.8, f32[3072]{0:T(1024)S(1)} %copy-done.60, f32[512,3072]{1,0:T(8,128)} %get-tuple-element.135), kind=kLoop, calls=%fused_computation.45 | loop fusion | flops 42467328 | bytes 18886656 | tf_op jit(solution)/shard_map/convert_element_type | solution.py:179
  313.5 4.7 copy.84
  318.3 4.8 convolution_bitcast_fusion.2
  323.1 12.7 %copy.86 = f32[16,2,384,192]{2,1,0,3:T(2,128)} copy(f32[16,2,384,192]{2,3,0,1:T(8,128)S(1)} %convolution_bitcast_fusion.2) | data formatting | bytes 18874368 | tf_op jit(solution)/shard_map/transpose | solution.py:64
  335.8 12.5 %reshape.1486 = f32[12288,192]{0,1:T(8,128)} reshape(f32[16,2,384,192]{2,1,0,3:T(2,128)} %copy.86) | data formatting | bytes 18874368 | tf_op jit(solution)/shard_map/reshape | solution.py:65
  348.4 2.3 copy.87
  350.8 4.8 copy.99
  355.6 4.7 convolution_bitcast_fusion
  360.3 11.1 %copy.89 = f32[16,2,1536,48]{2,1,0,3:T(2,128)} copy(f32[16,2,1536,48]{2,3,0,1:T(8,128)S(1)} %convolution_bitcast_fusion) | data formatting | bytes 18874368 | tf_op jit(solution)/shard_map/transpose | solution.py:64
  371.4 12.2 %reshape.1487 = f32[49152,48]{0,1:T(8,128)} reshape(f32[16,2,1536,48]{2,1,0,3:T(2,128)} %copy.89) | data formatting | bytes 18874368 | tf_op jit(solution)/shard_map/reshape | solution.py:65
  383.7 2.3 copy.97
  386.1 1.8 pad_maximum_fusion
  387.9 4.3 convolution_bitcast_fusion.3
  392.2 11.4 %copy.81 = f32[16,2,384,144]{2,1,0,3:T(2,128)} copy(f32[16,2,384,144]{2,3,0,1:T(8,128)} %convolution_bitcast_fusion.3) | data formatting | bytes 14155776 | tf_op jit(solution)/shard_map/transpose | solution.py:64
  403.6 9.8 %reshape.1484 = f32[12288,144]{0,1:T(8,128)} reshape(f32[16,2,384,144]{2,1,0,3:T(2,128)} %copy.81) | data formatting | bytes 14155776 | tf_op jit(solution)/shard_map/reshape | solution.py:65
  414.2 3.8 concatenate.72
  418.0 8.5 psum.14
  426.5 60.9 %psum.15 = f32[9988]{0:T(1024)} all-reduce(f32[9988]{0:T(1024)} %psum.14), channel_id=1, replica_groups=mesh['dp'=16,'seq'=2] {'dp'}, use_global_device_ids=true, to_apply=%region_27.28 | all-reduce | flops 9988 | bytes 79904 | tf_op jit(solution)/shard_map/psum | solution.py:339
  494.5 136.1 %reduce-scatter.18.cloned.1.call-done = f32[384,192]{0,1:T(8,128)} async-done(((f32[12288,192]{0,1:T(8,128)}), f32[384,192]{0,1:T(8,128)}) %reduce-scatter.18.cloned.1.call-update) | async-done | bytes 294928 | tf_op jit(solution)/shard_map/reduce_scatter | solution.py:366
  630.6 142.8 %reduce-scatter.20.cloned.1.call-done = f32[1536,48]{0,1:T(8,128)} async-done(((f32[49152,48]{0,1:T(8,128)}), f32[1536,48]{0,1:T(8,128)}) %reduce-scatter.20.cloned.1.call-update) | async-done | bytes 294928 | tf_op jit(solution)/shard_map/reduce_scatter | solution.py:372
  773.4 125.3 %reduce-scatter.14.cloned.1.call-done = f32[384,144]{0,1:T(8,128)} async-done(((f32[12288,144]{0,1:T(8,128)}), f32[384,144]{0,1:T(8,128)}) %reduce-scatter.14.cloned.1.call-update) | async-done | bytes 221200 | tf_op jit(solution)/shard_map/reduce_scatter | solution.py:354
  (228 shorter events, 60.6 us)
Async XLA Ops:
  7.2 36.1 %copy-start = (bf16[768,2304]{1,0:T(8,128)(2,1)S(1)}, bf16[768,2304]{1,0:T(8,128)(2,1)}, u32[]{:S(2)}) copy-start(bf16[768,2304]{1,0:T(8,128)(2,1)} %param.22) | copy-start | bytes 10616836
  7.2 87.1 %all-gather.5.cloned.1.call-start = ((), (), s32[]{:S(2)}) async-start(), calls=%async_computation.8 | async-start | bytes 2359296 | tf_op jit(solution)/shard_map/all_gather | solution.py:135
  11.4 31.4 %copy-start.41 = (f32[512]{0:T(512)}, f32[512]{0:T(512)S(1)}, u32[]{:S(2)}) copy-start(f32[512]{0:T(512)S(1)} %broadcast_multiply_fusion.4) | copy-start | bytes 6148
  13.5 29.3 %copy-start.45 = (f32[512]{0:T(512)}, f32[512]{0:T(512)S(1)}, u32[]{:S(2)}) copy-start(f32[512]{0:T(512)S(1)} %fusion.84) | copy-start | bytes 6148
  18.6 3.1 copy-start.51
  36.2 6.6 copy-start.5
  36.2 6.6 copy-start.43
  42.8 3.6 copy-start.2
  43.3 3.3 copy-start.23
  46.6 2.1 copy-start.20
  64.2 2.7 copy-start.40
  64.2 3.3 copy-start.48
  64.2 60.6 %all-gather.3.cloned.1.call-start = ((), (), s32[]{:S(2)}) async-start(), calls=%async_computation.7 | async-start | bytes 2359296 | tf_op jit(solution)/shard_map/all_gather | solution.py:136
  66.7 198.3 %reduce-scatter.8.cloned.1.call-start = ((), (), s32[]{:S(2)}) async-start(), calls=%async_computation.9 | async-start | bytes 2359296 | tf_op jit(solution)/shard_map/reduce_scatter | solution.py:277
  68.1 4.7 copy-start.61
  68.1 4.7 copy-start.62
  71.2 2.9 copy-start.9
  71.2 2.9 copy-start.28
  71.2 2.9 copy-start.31
  97.0 14.8 %copy-start.15 = (pred[512,1024]{1,0:T(8,128)(4,1)S(1)}, pred[512,1024]{1,0:T(8,128)(4,1)}, u32[]{:S(2)}) copy-start(pred[512,1024]{1,0:T(8,128)(4,1)} %compare_and_fusion) | copy-start | bytes 1572868
  111.8 11.8 %copy-start.38 = (f32[12,512]{1,0:T(8,128)}, f32[12,512]{1,0:T(8,128)S(1)}, u32[]{:S(2)}) copy-start(f32[12,512]{1,0:T(8,128)S(1)} %get-tuple-element.132) | copy-start | bytes 73732
  127.4 16.3 %slice-start = ((s8[9437184]{0:T(1024)(128)(4,1)}), s8[4194304]{0:T(1024)(128)(4,1)S(1)}, s32[]{:S(2)}) async-start(s8[9437184]{0:T(1024)(128)(4,1)} %bitcast.271), calls=%async_computation.16 | async-start | bytes 8388608
  127.4 13.2 %copy-start.6 = (bf16[1,512,768]{2,1,0:T(8,128)(2,1)S(1)}, bf16[1,512,768]{2,1,0:T(8,128)(2,1)}, u32[]{:S(2)}) copy-start(bf16[1,512,768]{2,1,0:T(8,128)(2,1)} %param.15) | copy-start | bytes 2359300
  127.4 13.2 %copy-start.34 = (bf16[768,768]{1,0:T(8,128)(2,1)S(1)}, bf16[768,768]{1,0:T(8,128)(2,1)}, u32[]{:S(2)}) copy-start(bf16[768,768]{1,0:T(8,128)(2,1)} %param.23) | copy-start | bytes 3538948
  127.4 16.3 %slice-start.1 = ((s8[9437184]{0:T(1024)(128)(4,1)}), s8[4194304]{0:T(1024)(128)(4,1)S(1)}, s32[]{:S(2)}) async-start(s8[9437184]{0:T(1024)(128)(4,1)} %bitcast.271), calls=%async_computation.17 | async-start | bytes 8388608
  127.4 16.3 %slice-start.2 = ((s8[9437184]{0:T(1024)(128)(4,1)}), s8[1048576]{0:T(1024)(128)(4,1)S(1)}, s32[]{:S(2)}) async-start(s8[9437184]{0:T(1024)(128)(4,1)} %bitcast.271), calls=%async_computation.18 | async-start | bytes 2097152
  140.6 2.7 copy-start.26
  140.6 3.1 copy-start.16
  140.6 3.1 copy-start.47
  140.7 4.4 slice-start.3
  143.3 21.7 %copy-start.21 = (f32[512,768]{1,0:T(8,128)}, f32[512,768]{1,0:T(8,128)S(1)}, u32[]{:S(2)}) copy-start(f32[512,768]{1,0:T(8,128)S(1)} %get-tuple-element.134) | copy-start | bytes 4718596
  143.4 29.3 %copy-start.3 = (f32[1,512,768]{2,1,0:T(8,128)}, f32[1,512,768]{2,1,0:T(8,128)S(1)}, u32[]{:S(2)}) copy-start(f32[1,512,768]{2,1,0:T(8,128)S(1)} %get-tuple-element.94) | copy-start | bytes 4718596
  143.4 1.7 slice-start.4
  143.8 4.0 slice-start.5
  145.0 2.7 copy-start.19
  145.1 7.9 copy-start.24
  145.1 2.7 copy-start.59
  145.1 2.8 slice-start.6
  147.9 5.1 copy-start.8
  153.0 12.1 %copy-start.64 = (f32[768]{0:T(1024)S(1)}, f32[768]{0:T(1024)}, u32[]{:S(2)}) copy-start(f32[768]{0:T(1024)} %param.28) | copy-start | bytes 9220
  173.8 2.1 copy-start.35
  198.7 17.6 %copy-start.18 = (bf16[512,12,64]{0,2,1:T(8,128)(2,1)S(1)}, bf16[512,12,64]{0,2,1:T(8,128)(2,1)}, u32[]{:S(2)}) copy-start(bf16[512,12,64]{0,2,1:T(8,128)(2,1)} %fusion.57) | copy-start | bytes 2359300
  216.3 5.1 copy-start.1
  221.4 54.8 %reduce-scatter.10.cloned.1.call-start = ((), (), s32[]{:S(2)}) async-start(), calls=%async_computation.10 | async-start | bytes 2359296 | tf_op jit(solution)/shard_map/reduce_scatter | solution.py:280
  235.1 259.4 %reduce-scatter.16.cloned.1.call-start = ((), (), s32[]{:S(2)}) async-start(), calls=%async_computation.13 | async-start | bytes 2433024 | tf_op jit(solution)/shard_map/reduce_scatter | solution.py:360
  250.0 10.3 %copy-start.37 = (f32[512,64]{0,1:T(8,128)S(1)}, f32[512,64]{0,1:T(8,128)}, u32[]{:S(2)}) copy-start(f32[512,64]{0,1:T(8,128)} %get-tuple-element.114) | copy-start | bytes 393220
  261.8 232.7 %reduce-scatter.12.cloned.1.call-start = ((), (), s32[]{:S(2)}) async-start(), calls=%async_computation.11 | async-start | bytes 3244032 | tf_op jit(solution)/shard_map/reduce_scatter | solution.py:348
  276.2 3.7 copy-start.7
  276.2 3.7 copy-start.42
  276.2 3.8 copy-start.44
  276.2 3.8 copy-start.46
  279.9 2.4 copy-start.50
  280.0 3.8 copy-start.13
  280.0 3.8 copy-start.17
  280.0 3.8 copy-start.22
  280.0 3.8 copy-start.55
  283.8 2.0 copy-start.11
  285.8 1.9 copy-start.33
  289.8 6.1 copy-start.58
  300.1 2.4 copy-start.60
  300.1 330.5 %reduce-scatter.18.cloned.1.call-start = ((), (), s32[]{:S(2)}) async-start(), calls=%async_computation.14 | async-start | bytes 9732096 | tf_op jit(solution)/shard_map/reduce_scatter | solution.py:366
  348.4 425.0 %reduce-scatter.20.cloned.1.call-start = ((), (), s32[]{:S(2)}) async-start(), calls=%async_computation.15 | async-start | bytes 9732096 | tf_op jit(solution)/shard_map/reduce_scatter | solution.py:372
  383.7 515.0 %reduce-scatter.14.cloned.1.call-start = ((), (), s32[]{:S(2)}) async-start(), calls=%async_computation.12 | async-start | bytes 7299072 | tf_op jit(solution)/shard_map/reduce_scatter | solution.py:354
  386.1 1.8 copy-start.36
  (18 other events, 18.9 us)
Sparse Core Ops, SparseCore 0:
  64.4 29.8 all-gather.4
  96.4 27.2 all-gather.2
  221.5 26.3 reduce-scatter.7
  250.1 26.0 reduce-scatter.9
  281.9 99.1 reduce-scatter.15
  387.8 100.5 reduce-scatter.11
  495.8 134.7 reduce-scatter.17
  637.1 136.2 reduce-scatter.19
  780.6 118.0 reduce-scatter.13
